TPU v7x, 32 devices: a whole 2x2x4 slice. The times are simulated.
32 devices in a mesh: dp: 8 (over y, x, core), ctx: 4 (over z).
Axes of the slice: x: 2, y: 2, z: 4, core: 2. Of those that a mesh axis runs over, the one named last changes fastest.
Arguments:
- inputs: bfloat16 [8, 512, 2048], P('dp', 'ctx'), may hold values from -6 to 6
- segment: int32 [8, 512], P('dp', 'ctx'), may hold values from 0 to 3, as said below
- w_qkv: bfloat16 [2048, 6144], P(('dp', 'ctx')), may hold values from -0.125 to 0.125
- w_out: bfloat16 [2048, 2048], P(('dp', 'ctx')), may hold values from -0.125 to 0.125
- w_gate: bfloat16 [2048, 8192], P('dp', 'ctx'), may hold values from -0.125 to 0.125
- w_up: bfloat16 [2048, 8192], P('dp', 'ctx'), may hold values from -0.125 to 0.125
- w_down_t: bfloat16 [2048, 8192], P('dp', 'ctx'), may hold values from -0.0625 to 0.0625
- gains: float32 [4, 2048], replicated, may hold values from 0.25 to 1.75
- cotangent: bfloat16 [8, 512, 2048], P('dp', 'ctx'), may hold values from -6 to 6
Outputs:
- output: bfloat16 [8, 512, 2048], P('dp', 'ctx')
- input_grad: float32 [8, 512, 2048], P('dp', 'ctx')
- grad_qkv: float32 [2048, 6144], P(('dp', 'ctx'))
- grad_out: float32 [2048, 2048], P(('dp', 'ctx'))
- grad_gate: float32 [2048, 8192], P('dp', 'ctx')
- grad_up: float32 [2048, 8192], P('dp', 'ctx')
- grad_down_t: float32 [2048, 8192], P('dp', 'ctx')
- grad_gains: float32 [4, 2048], replicated
Inputs may be any that keep to these rules, and one draw needn't show every extreme that they name: `segment`: in every sequence ids 1, 2 and 3 mark three documents in this order, each of one position or more, and 0 marks padding, one position or more at the sequence's end.
All inputs are finite; a program needn't handle non-finite values.
Results may differ from a plain program's by a relative error of at most 0.015.
Values may be sent and summed in bfloat16 or wider, within the bound.
A program may use at most 704 MiB of HBM per device.

v0:
```python
import jax
import jax.numpy as jnp
from jax import lax
from jax.sharding import Mesh
from jax.sharding import PartitionSpec as P

HEAD_DIM = 128
EPS = 1e-06
ROPE_BASE = 500000.0
F32 = jnp.float32
BF16 = jnp.bfloat16
GROUP = ("core", "ctx")
ALL = ("chip", "core", "ctx")


def rope_tables(positions):
    half = HEAD_DIM // 2
    frequency = ROPE_BASE ** (-(jnp.arange(half, dtype=F32) * 2.0 / HEAD_DIM))
    angles = positions[:, None] * frequency[None, :]
    cosine = jnp.cos(angles)
    sine = jnp.sin(angles)
    return (jnp.concatenate([cosine, cosine], 1), jnp.concatenate([sine, sine], 1))


def rotate(values, cosine, sine):
    half = HEAD_DIM // 2
    turned = jnp.concatenate([-values[..., half:], values[..., :half]], -1)
    return values * cosine + turned * sine


def rotate_back(values, cosine, sine):
    half = HEAD_DIM // 2
    scaled = values * sine
    turned = jnp.concatenate([scaled[..., half:], -scaled[..., :half]], -1)
    return values * cosine + turned


def dot(left, right):
    return jnp.dot(left, right, preferred_element_type=F32)


def dot_rows(left, right):
    return lax.dot_general(left, right, (((1,), (1,)), ((), ())), preferred_element_type=F32)


def dot_first(left, right):
    return lax.dot_general(left, right, (((0,), (0,)), ((), ())), preferred_element_type=F32)


def gather(values, axes):
    return lax.all_gather(values, axes, axis=0, tiled=True)


def scatter_sum(values, axes):
    return lax.psum_scatter(values, axes, scatter_dimension=0, tiled=True)


def norm_factor(values):
    return lax.rsqrt(jnp.mean(values * values, axis=-1, keepdims=True) + EPS)


def norm_back(values, factor, gain, grad):
    normed = values * factor
    scaled = gain * grad
    back = factor * (scaled - normed * jnp.mean(scaled * normed, axis=-1, keepdims=True))
    return (back, jnp.sum(grad * normed, axis=0))


def per_device(inputs, segment, w_qkv, w_out, w_gate, w_up, w_down_t, gains, cotangent):
    rows, width = inputs.shape[1:]
    cores = lax.axis_size("core")
    spans = lax.axis_size("ctx")
    members = cores * spans
    length = rows * spans
    total_rows = cores * length
    part = width // members
    heads = part // HEAD_DIM
    member = lax.axis_index(GROUP)
    tokens = inputs[0]
    qkv_rows = w_qkv.shape[0]
    qkv_cut = w_qkv.reshape(qkv_rows, 3, members, part).transpose(2, 0, 1, 3)
    qkv_cut = qkv_cut.reshape(members, qkv_rows, 3 * part)
    qkv_cut = lax.all_to_all(qkv_cut, GROUP, 0, 0, tiled=True)
    qkv_w = gather(qkv_cut.reshape(members * qkv_rows, 3 * part), "chip")
    tokens_all = gather(tokens, GROUP)
    out_full = gather(w_out, ALL)
    out_w = lax.dynamic_slice_in_dim(out_full, member * part, part, 0)
    hidden = w_gate.shape[1] // cores
    gate_up = jnp.concatenate(
        [w_gate.reshape(-1, cores, 1, hidden), w_up.reshape(-1, cores, 1, hidden)], 2
    ).reshape(-1, cores * 2 * hidden)
    gate_up = lax.all_to_all(gate_up, "core", 1, 0, tiled=True)
    gate_up_w = gather(gate_up, "chip")
    down_w = gather(lax.all_to_all(w_down_t, "core", 1, 0, tiled=True), "chip")
    mixed = dot(tokens_all, qkv_w)
    query_raw = mixed[:, :part]
    key_raw = mixed[:, part : 2 * part]
    value_low = mixed[:, 2 * part :].astype(BF16)
    squares = jnp.stack([jnp.sum(query_raw * query_raw, 1), jnp.sum(key_raw * key_raw, 1)])
    squares = lax.psum(squares, GROUP)
    factors = lax.rsqrt(squares / width + EPS)
    gain_q = lax.dynamic_slice_in_dim(gains[0], member * part, part)
    gain_k = lax.dynamic_slice_in_dim(gains[1], member * part, part)
    places = jnp.arange(length, dtype=jnp.int32)
    cosine, sine = rope_tables(places.astype(F32))
    cosine, sine = (cosine[None, :, None, :], sine[None, :, None, :])
    shape = (cores, length, heads, HEAD_DIM)
    query_factor, key_factor = (factors[0][:, None], factors[1][:, None])
    query_low = rotate((query_raw * query_factor * gain_q).reshape(shape), cosine, sine).astype(
        BF16
    )
    key_low = rotate((key_raw * key_factor * gain_k).reshape(shape), cosine, sine).astype(BF16)
    value_low = value_low.reshape(shape)
    ids = gather(segment[0], GROUP).reshape(cores, length)
    allowed = (
        (ids[:, :, None] == ids[:, None, :])
        & (places[None, None, :] <= places[None, :, None])
        & ((ids[:, None, :] != 0) | (places[None, None, :] == places[None, :, None]))
    )[:, None]
    scale = HEAD_DIM ** (-0.5)
    scores = jnp.einsum("bqhd,bkhd->bhqk", query_low, key_low, preferred_element_type=F32) * scale
    masked = jnp.where(allowed, scores, -1e30)
    row_max = jnp.max(masked, axis=-1, keepdims=True)
    weights = jnp.where(allowed, jnp.exp(masked - row_max), 0.0)
    shares = weights / jnp.sum(weights, axis=-1, keepdims=True)
    shares_low = shares.astype(BF16)
    attended = jnp.einsum("bhqk,bkhd->bqhd", shares_low, value_low, preferred_element_type=F32)
    attended_low = attended.reshape(total_rows, part).astype(BF16)
    projected = scatter_sum(dot(attended_low, out_w).astype(BF16), GROUP).astype(F32)
    tokens_wide = tokens.astype(F32)
    proj_factor = norm_factor(projected)
    residual = tokens_wide + projected * proj_factor * gains[2]
    residual_all = gather(residual.astype(BF16), GROUP)
    gate_up_out = dot(residual_all, gate_up_w)
    gate, up_part = (gate_up_out[:, :hidden], gate_up_out[:, hidden:])
    sigmoid = 1.0 / (1.0 + jnp.exp(-gate))
    activated = (gate * sigmoid * up_part).astype(BF16)
    feed = scatter_sum(dot_rows(activated, down_w).astype(BF16), GROUP).astype(F32)
    feed_factor = norm_factor(feed)
    output = (residual + feed * feed_factor * gains[3]).astype(BF16)
    upstream = cotangent[0].astype(F32)
    feed_grad, gain_feed = norm_back(feed, feed_factor, gains[3], upstream)
    feed_grad_all = gather(feed_grad.astype(BF16), GROUP)
    act_grad = dot(feed_grad_all, down_w)
    gate_grad = act_grad * up_part * sigmoid * (1.0 + gate * (1.0 - sigmoid))
    up_grad = act_grad * (gate * sigmoid)
    gate_up_grad = jnp.concatenate([gate_grad.astype(BF16), up_grad.astype(BF16)], 1)
    back_feed = scatter_sum(dot_rows(gate_up_grad, gate_up_w).astype(BF16), GROUP).astype(F32)
    residual_grad = upstream + back_feed
    grad_gate_up = scatter_sum(dot_first(residual_all, gate_up_grad).astype(BF16), "chip")
    grad_gate_up = lax.all_to_all(grad_gate_up, "core", 0, 1, tiled=True)
    grad_gate_up = grad_gate_up.reshape(-1, cores, 2, hidden).astype(F32)
    grad_gate = grad_gate_up[:, :, 0].reshape(-1, cores * hidden)
    grad_up = grad_gate_up[:, :, 1].reshape(-1, cores * hidden)
    grad_down = scatter_sum(dot_first(feed_grad_all, activated).astype(BF16), "chip")
    grad_down = lax.all_to_all(grad_down, "core", 0, 1, tiled=True).astype(F32)
    projected_grad, gain_attn = norm_back(projected, proj_factor, gains[2], residual_grad)
    projected_all = gather(projected_grad.astype(BF16), GROUP)
    attended_grad = dot_rows(projected_all, out_w).astype(BF16).reshape(shape)
    share_grad = jnp.einsum("bqhd,bkhd->bhqk", attended_grad, value_low, preferred_element_type=F32)
    inner = jnp.sum(shares * share_grad, axis=-1, keepdims=True)
    score_grad = (shares * (share_grad - inner)).astype(BF16)
    query_grad = jnp.einsum("bhqk,bkhd->bqhd", score_grad, key_low, preferred_element_type=F32)
    key_grad = jnp.einsum("bhqk,bqhd->bkhd", score_grad, query_low, preferred_element_type=F32)
    value_grad = jnp.einsum(
        "bhqk,bqhd->bkhd", shares_low, attended_grad, preferred_element_type=F32
    )
    query_turn = rotate_back(query_grad * scale, cosine, sine).reshape(total_rows, part)
    key_turn = rotate_back(key_grad * scale, cosine, sine).reshape(total_rows, part)
    query_norm, key_norm = (query_raw * query_factor, key_raw * key_factor)
    sums = jnp.stack(
        [jnp.sum(gain_q * query_turn * query_norm, 1), jnp.sum(gain_k * key_turn * key_norm, 1)]
    )
    means = lax.psum(sums, GROUP) / width
    query_mixed = query_factor * (gain_q * query_turn - query_norm * means[0][:, None])
    key_mixed = key_factor * (gain_k * key_turn - key_norm * means[1][:, None])
    gain_query = jnp.sum(query_turn * query_norm, 0)
    gain_key = jnp.sum(key_turn * key_norm, 0)
    mixed_grad = jnp.concatenate(
        [query_mixed, key_mixed, value_grad.reshape(total_rows, part)], 1
    ).astype(BF16)
    input_part = dot_rows(mixed_grad, qkv_w).astype(BF16)
    input_grad = residual_grad + scatter_sum(input_part, GROUP).astype(F32)
    grad_qkv = scatter_sum(dot_first(tokens_all, mixed_grad).astype(BF16), "chip")
    grad_qkv = grad_qkv.reshape(members, qkv_rows, 3 * part)
    grad_qkv = lax.all_to_all(grad_qkv, GROUP, 0, 0, tiled=True)
    grad_qkv = grad_qkv.reshape(members, qkv_rows, 3, part).transpose(1, 2, 0, 3)
    grad_qkv = grad_qkv.reshape(qkv_rows, 3 * width).astype(F32)
    out_part = dot_first(attended_low, projected_all).astype(BF16)
    out_part = lax.dynamic_update_slice_in_dim(
        jnp.zeros((width, width), BF16), out_part, member * part, 0
    )
    grad_out = scatter_sum(out_part, ALL).astype(F32)
    wide = jnp.zeros((2, width), F32)
    wide = lax.dynamic_update_slice(wide, jnp.stack([gain_query, gain_key]), (0, member * part))
    grad_gains = lax.psum(jnp.concatenate([wide, gain_attn[None], gain_feed[None]]), ALL)
    return (
        output[None],
        input_grad[None],
        grad_qkv,
        grad_out,
        grad_gate,
        grad_up,
        grad_down,
        grad_gains,
    )


def solution(mesh):
    cores = 2
    chips = mesh.shape["dp"] // cores
    split = Mesh(mesh.devices.reshape(chips, cores, mesh.shape["ctx"]), ALL)
    dp = ("chip", "core")
    every = P((*dp, "ctx"), None)
    in_specs = (
        P(dp, "ctx", None),
        P(dp, "ctx"),
        every,
        every,
        P(dp, "ctx"),
        P(dp, "ctx"),
        P(dp, "ctx"),
        P(),
        P(dp, "ctx", None),
    )
    out_specs = (
        P(dp, "ctx", None),
        P(dp, "ctx", None),
        every,
        every,
        P(dp, "ctx"),
        P(dp, "ctx"),
        P(dp, "ctx"),
        P(),
    )
    return jax.shard_map(
        per_device, mesh=split, in_specs=in_specs, out_specs=out_specs, check_vma=False
    )
```

profile of v0, /device:TPU:0, one launch (start us, length us, event | category | flops | bytes accessed | tf_op | source)
XLA Modules:
  0.0 1303.3 jit_solution(13197521999439722919)
XLA Ops:
  9.9 26.9 %all_to_all.74 = bf16[8,64,768]{2,1,0:T(8,128)(2,1)} all-to-all(bf16[8,64,768]{2,1,0:T(8,128)(2,1)S(1)} %reshape.177), channel_id=1, replica_groups=mesh['chip'=4,'core'=2,'ctx'=4] {'core','ctx'}, dimensions={0} | all-to-all | bytes 1572864 | tf_op jit(solution)/shard_map/all_to_all | solution.py:83
  38.3 12.7 all-gather.1
  55.5 23.9 %all-gather.11.cloned.1.call-done = bf16[2048,768]{1,0:T(8,128)(2,1)} async-done(((bf16[512,768]{1,0:T(8,128)(2,1)}), bf16[2048,768]{1,0:T(8,128)(2,1)}) %all-gather.11.cloned.1.call-update) | async-done | bytes 3145744 | tf_op jit(solution)/shard_map/all_gather | solution.py:51
  79.3 48.8 %all-gather.25.cloned.1.call-done = bf16[1,1024,2048]{2,1,0:T(8,128)(2,1)} async-done(((bf16[1,128,2048]{2,1,0:T(8,128)(2,1)}), bf16[1,1024,2048]{2,1,0:T(8,128)(2,1)}) %all-gather.25.cloned.1.call-update) | async-done | bytes 4194320 | tf_op jit(solution)/shard_map/all_gather | solution.py:51
  135.4 15.6 %psum.21 = f32[2,1024]{1,0:T(2,128)S(1)} all-reduce(f32[2,1024]{1,0:T(2,128)S(1)} %pad_maximum_fusion.10), channel_id=1, replica_groups=mesh['chip'=4,'core'=2,'ctx'=4] {'core','ctx'}, use_global_device_ids=true, to_apply=%region_2.0 | all-reduce | flops 2048 | bytes 16384 | tf_op jit(solution)/shard_map/psum | solution.py:100
  184.5 23.1 %all-gather.13.cloned.1.call-done = bf16[2048,2048]{1,0:T(8,128)(2,1)} async-done(((bf16[64,2048]{1,0:T(8,128)(2,1)}), bf16[2048,2048]{1,0:T(8,128)(2,1)}) %all-gather.13.cloned.1.call-update) | async-done | bytes 8388624 | tf_op jit(solution)/shard_map/all_gather | solution.py:51
  228.9 71.0 %reduce-scatter.9.cloned.1.call-done = bf16[128,2048]{1,0:T(8,128)(2,1)} async-done(((bf16[1024,2048]{1,0:T(8,128)(2,1)}), bf16[128,2048]{1,0:T(8,128)(2,1)}) %reduce-scatter.9.cloned.1.call-update) | async-done | bytes 524304 | tf_op jit(solution)/shard_map/reduce_scatter | solution.py:55
  315.1 74.5 %all-gather.17.cloned.1.call-done = bf16[2048,2048]{1,0:T(8,128)(2,1)} async-done(((bf16[512,2048]{1,0:T(8,128)(2,1)}), bf16[2048,2048]{1,0:T(8,128)(2,1)}) %all-gather.17.cloned.1.call-update) | async-done | bytes 8388624 | tf_op jit(solution)/shard_map/all_gather | solution.py:51
  389.6 49.2 %all-gather.15.cloned.1.call-done = bf16[1024,2048]{1,0:T(8,128)(2,1)} async-done(((bf16[128,2048]{1,0:T(8,128)(2,1)}), bf16[1024,2048]{1,0:T(8,128)(2,1)}) %all-gather.15.cloned.1.call-update) | async-done | bytes 4194320 | tf_op jit(solution)/shard_map/all_gather | solution.py:51
  438.8 12.5 fusion.74
  457.2 35.4 %all-gather.19.cloned.1.call-done = bf16[2048,1024]{1,0:T(8,128)(2,1)} async-done(((bf16[512,1024]{1,0:T(8,128)(2,1)}), bf16[2048,1024]{1,0:T(8,128)(2,1)}) %all-gather.19.cloned.1.call-update) | async-done | bytes 4194320 | tf_op jit(solution)/shard_map/all_gather | solution.py:51
  502.0 89.1 %reduce-scatter.11.cloned.1.call-done = bf16[128,2048]{1,0:T(8,128)(2,1)} async-done(((bf16[1024,2048]{1,0:T(8,128)(2,1)}), bf16[128,2048]{1,0:T(8,128)(2,1)}) %reduce-scatter.11.cloned.1.call-update) | async-done | bytes 524304 | tf_op jit(solution)/shard_map/reduce_scatter | solution.py:55
  596.6 46.8 %all-gather.21.cloned.1.call-done = bf16[1024,2048]{1,0:T(8,128)(2,1)} async-done(((bf16[128,2048]{1,0:T(8,128)(2,1)}), bf16[1024,2048]{1,0:T(8,128)(2,1)}) %all-gather.21.cloned.1.call-update) | async-done | bytes 4194320 | tf_op jit(solution)/shard_map/all_gather | solution.py:51
  643.4 11.6 multiply_convert_fusion.2
  657.1 12.7 convolution_convert_fusion.1
  669.8 87.8 %reduce-scatter.13.cloned.1.call-done = bf16[128,2048]{1,0:T(8,128)(2,1)} async-done(((bf16[1024,2048]{1,0:T(8,128)(2,1)}), bf16[128,2048]{1,0:T(8,128)(2,1)}) %reduce-scatter.13.cloned.1.call-update) | async-done | bytes 524304 | tf_op jit(solution)/shard_map/reduce_scatter | solution.py:55
  763.2 9.4 convolution_convert_fusion.4
  772.6 14.0 %convolution_convert_fusion = bf16[2048,2048]{1,0:T(8,128)(2,1)} fusion(bf16[1024,2048]{1,0:T(8,128)(2,1)} %all-gather.15.cloned.1.call-done, bf16[1024,1024]{1,0:T(8,128)(2,1)} %copy-done.24, bf16[1024,1024]{1,0:T(8,128)(2,1)} %copy-done.23), kind=kOutput, calls=%fused_computation.1 | convolution fusion | flops 8602517504 | bytes 16777216 | tf_op jit(solution)/shard_map/dot_general | solution.py:47
  786.9 22.9 %all-gather.23.cloned.1.call-done = bf16[1024,2048]{1,0:T(8,128)(2,1)} async-done(((bf16[128,2048]{1,0:T(8,128)(2,1)}), bf16[1024,2048]{1,0:T(8,128)(2,1)}) %all-gather.23.cloned.1.call-update) | async-done | bytes 4194320 | tf_op jit(solution)/shard_map/all_gather | solution.py:51
  830.7 15.6 %psum.22 = f32[2,1024]{1,0:T(2,128)S(1)} all-reduce(f32[2,1024]{1,0:T(2,128)S(1)} %pad_maximum_fusion.11), channel_id=1, replica_groups=mesh['chip'=4,'core'=2,'ctx'=4] {'core','ctx'}, use_global_device_ids=true, to_apply=%region_15.16 | all-reduce | flops 2048 | bytes 16384 | tf_op jit(solution)/shard_map/psum | solution.py:174
  877.9 76.0 %reduce-scatter.21.cloned.1.call-done = bf16[512,2048]{1,0:T(8,128)(2,1)} async-done(((bf16[2048,2048]{1,0:T(8,128)(2,1)}), bf16[512,2048]{1,0:T(8,128)(2,1)}) %reduce-scatter.21.cloned.1.call-update) | async-done | bytes 2097168 | tf_op jit(solution)/shard_map/reduce_scatter | solution.py:55
  957.6 43.1 %reduce-scatter.17.cloned.1.call-done = bf16[512,768]{0,1:T(8,128)(2,1)} async-done(((bf16[2048,768]{0,1:T(8,128)(2,1)}), bf16[512,768]{0,1:T(8,128)(2,1)}) %reduce-scatter.17.cloned.1.call-update) | async-done | bytes 786448 | tf_op jit(solution)/shard_map/reduce_scatter | solution.py:55
  1007.6 64.0 %psum.23 = f32[4,2048]{1,0:T(4,128)} all-reduce(f32[4,2048]{1,0:T(4,128)S(1)} %pad_maximum_fusion.9), channel_id=1, replica_groups=mesh['chip'=4,'core'=2,'ctx'=4] {'chip','core','ctx'}, use_global_device_ids=true, to_apply=%region_25.26 | all-reduce | flops 8192 | bytes 65536 | tf_op jit(solution)/shard_map/psum | solution.py:196
  1108.9 185.7 %reduce-scatter.19.cloned.1.call-done = bf16[64,2048]{1,0:T(8,128)(2,1)} async-done(((bf16[2048,2048]{1,0:T(8,128)(2,1)}), bf16[64,2048]{1,0:T(8,128)(2,1)}) %reduce-scatter.19.cloned.1.call-update) | async-done | bytes 262160 | tf_op jit(solution)/shard_map/reduce_scatter | solution.py:55
  (189 shorter events, 216.2 us)
Async XLA Ops:
  7.2 72.2 %all-gather.11.cloned.1.call-start = ((), (), s32[]{:S(2)}) async-start(), calls=%async_computation.14 | async-start | bytes 3932160 | tf_op jit(solution)/shard_map/all_gather | solution.py:51
  7.2 31.1 %copy-start.21 = (s32[1,128]{1,0:T(1,128)S(1)}, s32[1,128]{1,0:T(1,128)}, u32[]{:S(2)}) copy-start(s32[1,128]{1,0:T(1,128)} %param.10) | copy-start | bytes 1540
  7.2 45.0 %copy-start.20 = (f32[4,2048]{1,0:T(4,128)S(1)}, f32[4,2048]{1,0:T(4,128)}, u32[]{:S(2)}) copy-start(f32[4,2048]{1,0:T(4,128)} %param.16) | copy-start | bytes 98308
  36.8 91.3 %all-gather.25.cloned.1.call-start = ((), (), s32[]{:S(2)}) async-start(), calls=%async_computation.29 | async-start | bytes 4718592 | tf_op jit(solution)/shard_map/all_gather | solution.py:51
  37.5 170.0 %all-gather.13.cloned.1.call-start = ((), (), s32[]{:S(2)}) async-start(), calls=%async_computation.15 | async-start | bytes 8650752 | tf_op jit(solution)/shard_map/all_gather | solution.py:51
  38.3 261.6 %reduce-scatter.9.cloned.1.call-start = ((), (), s32[]{:S(2)}) async-start(), calls=%async_computation.16 | async-start | bytes 4718592 | tf_op jit(solution)/shard_map/reduce_scatter | solution.py:55
  212.2 177.4 %all-gather.17.cloned.1.call-start = ((), (), s32[]{:S(2)}) async-start(), calls=%async_computation.18 | async-start | bytes 10485760 | tf_op jit(solution)/shard_map/all_gather | solution.py:51
  228.8 210.0 %all-gather.15.cloned.1.call-start = ((), (), s32[]{:S(2)}) async-start(), calls=%async_computation.17 | async-start | bytes 4718592 | tf_op jit(solution)/shard_map/all_gather | solution.py:51
  303.4 189.2 %all-gather.19.cloned.1.call-start = ((), (), s32[]{:S(2)}) async-start(), calls=%async_computation.19 | async-start | bytes 5242880 | tf_op jit(solution)/shard_map/all_gather | solution.py:51
  314.8 276.3 %reduce-scatter.11.cloned.1.call-start = ((), (), s32[]{:S(2)}) async-start(), calls=%async_computation.20 | async-start | bytes 4718592 | tf_op jit(solution)/shard_map/reduce_scatter | solution.py:55
  502.0 141.5 %all-gather.21.cloned.1.call-start = ((), (), s32[]{:S(2)}) async-start(), calls=%async_computation.21 | async-start | bytes 4718592 | tf_op jit(solution)/shard_map/all_gather | solution.py:51
  596.4 161.2 %reduce-scatter.13.cloned.1.call-start = ((), (), s32[]{:S(2)}) async-start(), calls=%async_computation.22 | async-start | bytes 4718592 | tf_op jit(solution)/shard_map/reduce_scatter | solution.py:55
  669.7 140.0 %all-gather.23.cloned.1.call-start = ((), (), s32[]{:S(2)}) async-start(), calls=%async_computation.23 | async-start | bytes 4718592 | tf_op jit(solution)/shard_map/all_gather | solution.py:51
  762.7 107.6 %reduce-scatter.23.cloned.1.call-start = ((), (), s32[]{:S(2)}) async-start(), calls=%async_computation.28 | async-start | bytes 5242880 | tf_op jit(solution)/shard_map/reduce_scatter | solution.py:55
  772.6 181.3 %reduce-scatter.21.cloned.1.call-start = ((), (), s32[]{:S(2)}) async-start(), calls=%async_computation.27 | async-start | bytes 10485760 | tf_op jit(solution)/shard_map/reduce_scatter | solution.py:55
  786.7 214.1 %reduce-scatter.17.cloned.1.call-start = ((), (), s32[]{:S(2)}) async-start(), calls=%async_computation.25 | async-start | bytes 3932160 | tf_op jit(solution)/shard_map/reduce_scatter | solution.py:55
  849.5 6.5 copy-start.19
  855.7 251.0 %reduce-scatter.15.cloned.1.call-start = ((), (), s32[]{:S(2)}) async-start(), calls=%async_computation.24 | async-start | bytes 4718592 | tf_op jit(solution)/shard_map/reduce_scatter | solution.py:55
  863.7 4.4 copy-start.6
  863.7 430.9 %reduce-scatter.19.cloned.1.call-start = ((), (), s32[]{:S(2)}) async-start(), calls=%async_computation.26 | async-start | bytes 8650752 | tf_op jit(solution)/shard_map/reduce_scatter | solution.py:55
  953.9 49.1 %all-to-all-start.4 = ((bf16[2,256,2048]{2,1,0:T(8,128)(2,1)}), bf16[2,256,2048]{2,1,0:T(8,128)(2,1)S(1)}, u32[]{:S(2)}, u32[]{:S(2)}) async-start(bf16[2,256,2048]{2,1,0:T(8,128)(2,1)} %bitcast.167), calls=%async_computation.11 | async-start | bytes 4194304 | tf_op jit(solution)/shard_map/all_to_all | solution.py:151
  1003.0 92.6 %all-to-all-start.3 = ((bf16[8,64,768]{2,1,0:T(8,128)(2,1)}), bf16[8,64,768]{2,1,0:T(8,128)(2,1)}, u32[]{:S(2)}, u32[]{:S(2)}) async-start(bf16[8,64,768]{2,1,0:T(8,128)(2,1)} %bitcast.33), calls=%async_computation.8 | async-start | bytes 1572864 | tf_op jit(solution)/shard_map/all_to_all | solution.py:186
  1095.6 11.0 copy-start
  1095.6 11.0 copy-start.8
  (19 other events, 45.7 us)
Sparse Core Ops, SparseCore 0:
  36.9 42.3 all-gather.10
  80.9 47.1 all-gather.24
  131.0 76.4 all-gather.12
  212.3 87.5 reduce-scatter.8
  302.2 87.3 all-gather.16
  391.6 47.1 all-gather.14
  441.2 51.4 all-gather.18
  502.1 88.9 reduce-scatter.10
  596.5 46.9 all-gather.20
  669.9 87.6 reduce-scatter.12
  762.9 46.8 all-gather.22
  812.6 51.4 reduce-scatter.22
  867.4 86.4 reduce-scatter.20
  956.7 43.9 reduce-scatter.16
  1002.9 103.7 reduce-scatter.14
  1108.8 185.7 reduce-scatter.18
where the time goes:
time: 1310 us; the launch traced here: 1300 us
  waiting for transfers between devices  885 us (68%)
  blocking collectives  153 us (12%)
  matrix products  116 us (9%)
  local copies, waits for them, and re-layouts  83.7 us (6%)
  other arithmetic  39.8 us (3%)
  between operations  14.9 us (1%)
    reduce_scatter x8, waiting for transfers between devices, scatter_sum(): return lax.psum_scatter(values, axes, scatter_dimension=0, tiled=True)  559 us
    all_gather x8, waiting for transfers between devices, gather(): return lax.all_gather(values, axes, axis=0, tiled=True)  325 us
    psum x1, blocking collectives, per_device(): lax.psum(jnp.concatenate([wide, gain_attn[None], gain_feed[None]]), ALL)  64 us
    dot_general x4, matrix products, dot(): return jnp.dot(left, right, preferred_element_type=F32)  34.9 us
    dot_general x4, matrix products, dot_rows(): lax.dot_general(left, right, (((1,), (1,)), ((), ())), preferred_element_...  34.2 us
    dot_general x4, matrix products, dot_first(): lax.dot_general(left, right, (((0,), (0,)), ((), ())), preferred_element_...  31.8 us
    all_to_all x1, blocking collectives, per_device(): qkv_cut = lax.all_to_all(qkv_cut, GROUP, 0, 0, tiled=True)  26.9 us
  transfers between devices with their start and end apart: 18, of which 15 were waited for; matrix products, arithmetic and copies ran while one was open for 14% of the time, Pallas kernels for 0%

commit v1 on v0

--- a/solution.py
+++ b/solution.py
@@ -193,7 +193,9 @@
     grad_out = scatter_sum(out_part, ALL).astype(F32)
     wide = jnp.zeros((2, width), F32)
     wide = lax.dynamic_update_slice(wide, jnp.stack([gain_query, gain_key]), (0, member * part))
-    grad_gains = lax.psum(jnp.concatenate([wide, gain_attn[None], gain_feed[None]]), ALL)
+    grad_gains = jnp.sum(
+        lax.all_gather(jnp.concatenate([wide, gain_attn[None], gain_feed[None]]), ALL), axis=0
+    )
     return (
         output[None],
         input_grad[None],

time: 1310 us -> 1360 us (1.038)
  waiting for transfers between devices: 885 us -> 993 us
  blocking collectives: 153 us -> 90.4 us
    reduce_scatter x8, waiting for transfers between devices: 559 us -> 626 us  [scatter_sum(): return lax.psum_scatter(values, axes, scatter_dimension=0, tiled=True)]
    psum x1 -> x0, blocking collectives: 64 us -> none  [per_device(): lax.psum(jnp.concatenate([wide, gain_attn[None], gain_feed[None]]), ALL)]
    all_gather x0 -> x1, waiting for transfers between devices: none -> 26 us  [per_device(): lax.all_gather(jnp.concatenate([wide, gain_attn[None], gain_feed[None]]),...]
    all_gather x8, waiting for transfers between devices: 325 us -> 339 us  [gather(): return lax.all_gather(values, axes, axis=0, tiled=True)]
  transfers between devices with their start and end apart: 18 -> 19, of which waited for: 15 -> 16; matrix products, arithmetic and copies ran while one was open for 14% -> 13% of each run, Pallas kernels for 0% -> 0%
where the time goes in v1:
time: 1360 us; the launch traced here: 1350 us
  waiting for transfers between devices  993 us (73%)
  matrix products  116 us (9%)
  blocking collectives  90.4 us (7%)
  local copies, waits for them, and re-layouts  84.3 us (6%)
  other arithmetic  42.4 us (3%)
  between operations  14.8 us (1%)
    reduce_scatter x8, waiting for transfers between devices, scatter_sum(): return lax.psum_scatter(values, axes, scatter_dimension=0, tiled=True)  626 us
    all_gather x8, waiting for transfers between devices, gather(): return lax.all_gather(values, axes, axis=0, tiled=True)  339 us
    dot_general x4, matrix products, dot(): return jnp.dot(left, right, preferred_element_type=F32)  34.9 us
    dot_general x4, matrix products, dot_rows(): lax.dot_general(left, right, (((1,), (1,)), ((), ())), preferred_element_...  33.5 us
    dot_general x4, matrix products, dot_first(): lax.dot_general(left, right, (((0,), (0,)), ((), ())), preferred_element_...  31.6 us
  transfers between devices with their start and end apart: 19, of which 16 were waited for; matrix products, arithmetic and copies ran while one was open for 13% of the time, Pallas kernels for 0%

profile of v1, /device:TPU:0, one launch (start us, length us, event | category | flops | bytes accessed | tf_op | source)
XLA Modules:
  0.0 1350.4 jit_solution(12712817487035756288)
XLA Ops:
  9.9 26.9 %all_to_all.74 = bf16[8,64,768]{2,1,0:T(8,128)(2,1)} all-to-all(bf16[8,64,768]{2,1,0:T(8,128)(2,1)S(1)} %reshape.177), channel_id=1, replica_groups=mesh['chip'=4,'core'=2,'ctx'=4] {'core','ctx'}, dimensions={0} | all-to-all | bytes 1572864 | tf_op jit(solution)/shard_map/all_to_all | solution.py:83
  38.3 12.7 all-gather.1
  55.4 23.9 %all-gather.14.cloned.1.call-done = bf16[2048,768]{1,0:T(8,128)(2,1)} async-done(((bf16[512,768]{1,0:T(8,128)(2,1)}), bf16[2048,768]{1,0:T(8,128)(2,1)}) %all-gather.14.cloned.1.call-update) | async-done | bytes 3145744 | tf_op jit(solution)/shard_map/all_gather | solution.py:51
  79.3 48.8 %all-gather.28.cloned.1.call-done = bf16[1,1024,2048]{2,1,0:T(8,128)(2,1)} async-done(((bf16[1,128,2048]{2,1,0:T(8,128)(2,1)}), bf16[1,1024,2048]{2,1,0:T(8,128)(2,1)}) %all-gather.28.cloned.1.call-update) | async-done | bytes 4194320 | tf_op jit(solution)/shard_map/all_gather | solution.py:51
  135.4 15.6 %psum.14 = f32[2,1024]{1,0:T(2,128)S(1)} all-reduce(f32[2,1024]{1,0:T(2,128)S(1)} %pad_maximum_fusion.9), channel_id=1, replica_groups=mesh['chip'=4,'core'=2,'ctx'=4] {'core','ctx'}, use_global_device_ids=true, to_apply=%region_2.0 | all-reduce | flops 2048 | bytes 16384 | tf_op jit(solution)/shard_map/psum | solution.py:100
  184.5 23.1 %all-gather.16.cloned.1.call-done = bf16[2048,2048]{1,0:T(8,128)(2,1)} async-done(((bf16[64,2048]{1,0:T(8,128)(2,1)}), bf16[2048,2048]{1,0:T(8,128)(2,1)}) %all-gather.16.cloned.1.call-update) | async-done | bytes 8388624 | tf_op jit(solution)/shard_map/all_gather | solution.py:51
  228.9 71.0 %reduce-scatter.9.cloned.1.call-done = bf16[128,2048]{1,0:T(8,128)(2,1)} async-done(((bf16[1024,2048]{1,0:T(8,128)(2,1)}), bf16[128,2048]{1,0:T(8,128)(2,1)}) %reduce-scatter.9.cloned.1.call-update) | async-done | bytes 524304 | tf_op jit(solution)/shard_map/reduce_scatter | solution.py:55
  315.1 74.5 %all-gather.20.cloned.1.call-done = bf16[2048,2048]{1,0:T(8,128)(2,1)} async-done(((bf16[512,2048]{1,0:T(8,128)(2,1)}), bf16[2048,2048]{1,0:T(8,128)(2,1)}) %all-gather.20.cloned.1.call-update) | async-done | bytes 8388624 | tf_op jit(solution)/shard_map/all_gather | solution.py:51
  389.6 49.2 %all-gather.18.cloned.1.call-done = bf16[1024,2048]{1,0:T(8,128)(2,1)} async-done(((bf16[128,2048]{1,0:T(8,128)(2,1)}), bf16[1024,2048]{1,0:T(8,128)(2,1)}) %all-gather.18.cloned.1.call-update) | async-done | bytes 4194320 | tf_op jit(solution)/shard_map/all_gather | solution.py:51
  438.8 12.5 fusion.74
  457.3 35.4 %all-gather.22.cloned.1.call-done = bf16[2048,1024]{1,0:T(8,128)(2,1)} async-done(((bf16[512,1024]{1,0:T(8,128)(2,1)}), bf16[2048,1024]{1,0:T(8,128)(2,1)}) %all-gather.22.cloned.1.call-update) | async-done | bytes 4194320 | tf_op jit(solution)/shard_map/all_gather | solution.py:51
  502.0 89.1 %reduce-scatter.11.cloned.1.call-done = bf16[128,2048]{1,0:T(8,128)(2,1)} async-done(((bf16[1024,2048]{1,0:T(8,128)(2,1)}), bf16[128,2048]{1,0:T(8,128)(2,1)}) %reduce-scatter.11.cloned.1.call-update) | async-done | bytes 524304 | tf_op jit(solution)/shard_map/reduce_scatter | solution.py:55
  596.7 46.8 %all-gather.24.cloned.1.call-done = bf16[1024,2048]{1,0:T(8,128)(2,1)} async-done(((bf16[128,2048]{1,0:T(8,128)(2,1)}), bf16[1024,2048]{1,0:T(8,128)(2,1)}) %all-gather.24.cloned.1.call-update) | async-done | bytes 4194320 | tf_op jit(solution)/shard_map/all_gather | solution.py:51
  643.5 11.6 multiply_convert_fusion.2
  657.1 12.6 convolution_convert_fusion.1
  669.8 87.8 %reduce-scatter.13.cloned.1.call-done = bf16[128,2048]{1,0:T(8,128)(2,1)} async-done(((bf16[1024,2048]{1,0:T(8,128)(2,1)}), bf16[128,2048]{1,0:T(8,128)(2,1)}) %reduce-scatter.13.cloned.1.call-update) | async-done | bytes 524304 | tf_op jit(solution)/shard_map/reduce_scatter | solution.py:55
  772.6 37.1 %all-gather.26.cloned.1.call-done = bf16[1024,2048]{1,0:T(8,128)(2,1)} async-done(((bf16[128,2048]{1,0:T(8,128)(2,1)}), bf16[1024,2048]{1,0:T(8,128)(2,1)}) %all-gather.26.cloned.1.call-update) | async-done | bytes 4194320 | tf_op jit(solution)/shard_map/all_gather | solution.py:51
  830.6 15.6 %psum.15 = f32[2,1024]{1,0:T(2,128)S(1)} all-reduce(f32[2,1024]{1,0:T(2,128)S(1)} %pad_maximum_fusion.10), channel_id=1, replica_groups=mesh['chip'=4,'core'=2,'ctx'=4] {'core','ctx'}, use_global_device_ids=true, to_apply=%region_15.16 | all-reduce | flops 2048 | bytes 16384 | tf_op jit(solution)/shard_map/psum | solution.py:174
  855.9 13.6 %convolution_convert_fusion = bf16[2048,2048]{1,0:T(8,128)(2,1)} fusion(bf16[1024,2048]{1,0:T(8,128)(2,1)} %all-gather.18.cloned.1.call-done, bf16[1024,1024]{1,0:T(8,128)(2,1)} %copy-done.27, bf16[1024,1024]{1,0:T(8,128)(2,1)S(1)} %copy-done.26), kind=kOutput, calls=%fused_computation.1 | convolution fusion | flops 8602517504 | bytes 16777216 | tf_op jit(solution)/shard_map/dot_general | solution.py:47
  888.6 22.7 %reduce-scatter.17.cloned.1.call-done = bf16[512,768]{0,1:T(8,128)(2,1)} async-done(((bf16[2048,768]{0,1:T(8,128)(2,1)}), bf16[512,768]{0,1:T(8,128)(2,1)}) %reduce-scatter.17.cloned.1.call-update) | async-done | bytes 786448 | tf_op jit(solution)/shard_map/reduce_scatter | solution.py:55
  913.6 87.4 %reduce-scatter.21.cloned.1.call-done = bf16[512,2048]{1,0:T(8,128)(2,1)} async-done(((bf16[2048,2048]{1,0:T(8,128)(2,1)}), bf16[512,2048]{1,0:T(8,128)(2,1)}) %reduce-scatter.21.cloned.1.call-update) | async-done | bytes 2097168 | tf_op jit(solution)/shard_map/reduce_scatter | solution.py:55
  1038.0 26.0 %all-gather.30.cloned.1.call-done = f32[32,4,2048]{2,1,0:T(4,128)} async-done(((f32[1,4,2048]{2,1,0:T(4,128)}), f32[32,4,2048]{2,1,0:T(4,128)}) %all-gather.30.cloned.1.call-update) | async-done | bytes 1048592 | tf_op jit(solution)/shard_map/all_gather | solution.py:197
  1071.2 83.0 %reduce-scatter.15.cloned.1.call-done = bf16[128,2048]{1,0:T(8,128)(2,1)} async-done(((bf16[1024,2048]{1,0:T(8,128)(2,1)}), bf16[128,2048]{1,0:T(8,128)(2,1)}) %reduce-scatter.15.cloned.1.call-update) | async-done | bytes 524304 | tf_op jit(solution)/shard_map/reduce_scatter | solution.py:55
  1156.4 185.5 %reduce-scatter.19.cloned.1.call-done = bf16[64,2048]{1,0:T(8,128)(2,1)} async-done(((bf16[2048,2048]{1,0:T(8,128)(2,1)}), bf16[64,2048]{1,0:T(8,128)(2,1)}) %reduce-scatter.19.cloned.1.call-update) | async-done | bytes 262160 | tf_op jit(solution)/shard_map/reduce_scatter | solution.py:55
  (198 shorter events, 223.3 us)
Async XLA Ops:
  7.2 72.2 %all-gather.14.cloned.1.call-start = ((), (), s32[]{:S(2)}) async-start(), calls=%async_computation.14 | async-start | bytes 3932160 | tf_op jit(solution)/shard_map/all_gather | solution.py:51
  7.2 31.1 %copy-start.23 = (s32[1,128]{1,0:T(1,128)S(1)}, s32[1,128]{1,0:T(1,128)}, u32[]{:S(2)}) copy-start(s32[1,128]{1,0:T(1,128)} %param.10) | copy-start | bytes 1540
  7.2 45.0 %copy-start.22 = (f32[4,2048]{1,0:T(4,128)S(1)}, f32[4,2048]{1,0:T(4,128)}, u32[]{:S(2)}) copy-start(f32[4,2048]{1,0:T(4,128)} %param.16) | copy-start | bytes 98308
  36.8 91.3 %all-gather.28.cloned.1.call-start = ((), (), s32[]{:S(2)}) async-start(), calls=%async_computation.29 | async-start | bytes 4718592 | tf_op jit(solution)/shard_map/all_gather | solution.py:51
  37.5 170.0 %all-gather.16.cloned.1.call-start = ((), (), s32[]{:S(2)}) async-start(), calls=%async_computation.15 | async-start | bytes 8650752 | tf_op jit(solution)/shard_map/all_gather | solution.py:51
  38.3 261.7 %reduce-scatter.9.cloned.1.call-start = ((), (), s32[]{:S(2)}) async-start(), calls=%async_computation.16 | async-start | bytes 4718592 | tf_op jit(solution)/shard_map/reduce_scatter | solution.py:55
  212.2 177.4 %all-gather.20.cloned.1.call-start = ((), (), s32[]{:S(2)}) async-start(), calls=%async_computation.18 | async-start | bytes 10485760 | tf_op jit(solution)/shard_map/all_gather | solution.py:51
  228.9 209.9 %all-gather.18.cloned.1.call-start = ((), (), s32[]{:S(2)}) async-start(), calls=%async_computation.17 | async-start | bytes 4718592 | tf_op jit(solution)/shard_map/all_gather | solution.py:51
  303.4 189.2 %all-gather.22.cloned.1.call-start = ((), (), s32[]{:S(2)}) async-start(), calls=%async_computation.19 | async-start | bytes 5242880 | tf_op jit(solution)/shard_map/all_gather | solution.py:51
  314.9 276.3 %reduce-scatter.11.cloned.1.call-start = ((), (), s32[]{:S(2)}) async-start(), calls=%async_computation.20 | async-start | bytes 4718592 | tf_op jit(solution)/shard_map/reduce_scatter | solution.py:55
  502.0 141.5 %all-gather.24.cloned.1.call-start = ((), (), s32[]{:S(2)}) async-start(), calls=%async_computation.21 | async-start | bytes 4718592 | tf_op jit(solution)/shard_map/all_gather | solution.py:51
  596.4 161.2 %reduce-scatter.13.cloned.1.call-start = ((), (), s32[]{:S(2)}) async-start(), calls=%async_computation.22 | async-start | bytes 4718592 | tf_op jit(solution)/shard_map/reduce_scatter | solution.py:55
  669.7 140.1 %all-gather.26.cloned.1.call-start = ((), (), s32[]{:S(2)}) async-start(), calls=%async_computation.23 | async-start | bytes 4718592 | tf_op jit(solution)/shard_map/all_gather | solution.py:51
  762.7 122.3 %reduce-scatter.23.cloned.1.call-start = ((), (), s32[]{:S(2)}) async-start(), calls=%async_computation.28 | async-start | bytes 5242880 | tf_op jit(solution)/shard_map/reduce_scatter | solution.py:55
  772.2 139.1 %reduce-scatter.17.cloned.1.call-start = ((), (), s32[]{:S(2)}) async-start(), calls=%async_computation.25 | async-start | bytes 3932160 | tf_op jit(solution)/shard_map/reduce_scatter | solution.py:55
  849.5 6.5 copy-start.26
  855.7 145.2 %reduce-scatter.21.cloned.1.call-start = ((), (), s32[]{:S(2)}) async-start(), calls=%async_computation.27 | async-start | bytes 10485760 | tf_op jit(solution)/shard_map/reduce_scatter | solution.py:55
  869.6 194.4 %all-gather.30.cloned.1.call-start = ((), (), s32[]{:S(2)}) async-start(), calls=%async_computation.30 | async-start | bytes 1081344 | tf_op jit(solution)/shard_map/all_gather | solution.py:197
  870.3 283.8 %reduce-scatter.15.cloned.1.call-start = ((), (), s32[]{:S(2)}) async-start(), calls=%async_computation.24 | async-start | bytes 4718592 | tf_op jit(solution)/shard_map/reduce_scatter | solution.py:55
  878.0 463.9 %reduce-scatter.19.cloned.1.call-start = ((), (), s32[]{:S(2)}) async-start(), calls=%async_computation.26 | async-start | bytes 8650752 | tf_op jit(solution)/shard_map/reduce_scatter | solution.py:55
  885.0 28.6 %all-to-all-start.5 = ((bf16[2,256,1024]{2,1,0:T(8,128)(2,1)}), bf16[2,256,1024]{2,1,0:T(8,128)(2,1)S(1)}, u32[]{:S(2)}, u32[]{:S(2)}) async-start(bf16[2,256,1024]{2,1,0:T(8,128)(2,1)} %bitcast.176), calls=%async_computation.13 | async-start | bytes 2097152 | tf_op jit(solution)/shard_map/all_to_all | solution.py:156
  1007.6 58.5 %all-to-all-start.3 = ((bf16[8,64,768]{2,1,0:T(8,128)(2,1)}), bf16[8,64,768]{2,1,0:T(8,128)(2,1)}, u32[]{:S(2)}, u32[]{:S(2)}) async-start(bf16[8,64,768]{2,1,0:T(8,128)(2,1)} %bitcast.169), calls=%async_computation.8 | async-start | bytes 1572864 | tf_op jit(solution)/shard_map/all_to_all | solution.py:186
  1066.0 88.1 %copy-start = (bf16[1,128,2048]{2,1,0:T(8,128)(2,1)S(1)}, bf16[1,128,2048]{2,1,0:T(8,128)(2,1)}, u32[]{:S(2)}) copy-start(bf16[1,128,2048]{2,1,0:T(8,128)(2,1)} %param.17) | copy-start | bytes 1572868
  1066.0 88.1 %copy-start.8 = (bf16[128,2048]{1,0:T(8,128)(2,1)S(1)}, bf16[128,2048]{1,0:T(8,128)(2,1)}, u32[]{:S(2)}) copy-start(bf16[128,2048]{1,0:T(8,128)(2,1)} %reduce-scatter.13.cloned.1.call-done) | copy-start | bytes 1572868
  (23 other events, 54.2 us)
Sparse Core Ops, SparseCore 0:
  36.9 42.3 all-gather.13
  80.9 47.1 all-gather.27
  131.0 76.4 all-gather.15
  212.3 87.5 reduce-scatter.8
  302.2 87.3 all-gather.19
  391.6 47.1 all-gather.17
  441.2 51.4 all-gather.21
  502.1 88.9 reduce-scatter.10
  596.5 46.8 all-gather.23
  669.9 87.6 reduce-scatter.12
  762.8 46.8 all-gather.25
  812.6 51.4 reduce-scatter.22
  867.3 43.9 reduce-scatter.16
  914.5 86.4 reduce-scatter.20
  1004.3 59.6 all-gather.29
  1066.2 87.9 reduce-scatter.14
  1156.3 185.5 reduce-scatter.18
